TPU v7x, 32 devices: a whole 2x2x4 slice. The times are simulated.
32 devices in a mesh: pb: 4 (over y, core), kv: 4 (over z), ex: 2 (over x).
Axes of the slice: x: 2, y: 2, z: 4, core: 2. Of those that a mesh axis runs over, the one named last changes fastest.
Arguments:
- queries: bfloat16 [8, 8192, 256], P(('pb', 'ex'), 'kv'), may hold values from -6 to 6
- coords: float32 [8, 3, 8192], P(('pb', 'ex'), None, 'kv'), may hold values from -1 to 1
- inputs: bfloat16 [8, 2048, 256], P(('pb', 'ex'), 'kv'), may hold values from -10 to 10
- w_query: bfloat16 [256, 256], replicated, may hold values from -0.375 to 0.375
- w_key: bfloat16 [256, 256], replicated, may hold values from -0.375 to 0.375
- w_value: bfloat16 [256, 256], replicated, may hold values from -0.375 to 0.375
- w_out: bfloat16 [256, 256], replicated, may hold values from -0.375 to 0.375
- expert_in: bfloat16 [8, 256, 1024], P('ex', ('pb', 'kv')), may hold values from -0.375 to 0.375
- expert_out: bfloat16 [8, 1024, 256], P('ex', ('pb', 'kv')), may hold values from -0.1875 to 0.1875
- gate_geo: float32 [8, 3], replicated, may hold values from -6 to 6
- routes: int32 [8, 64, 1], P(('pb', 'ex'), 'kv'), may hold values from 0 to 7; in each aligned block of 16 rows (0 to 15, 16 to 31, ..., all dimensions but the last counted through in order) at most 3 rows name the same one
Outputs:
- result: bfloat16 [8, 8192, 256], P(('pb', 'ex'), 'kv')
Inputs may be any that keep to these rules, and one draw needn't show every extreme that they name: `routes`: in each aligned block of 16 tiles (the tiles of one device) no expert is named by more than 3 tiles, a bound that some block reaches.
All inputs are finite; a program needn't handle non-finite values.
Results may differ from a plain program's by a relative error of at most 0.0053.
Values may be sent and summed in bfloat16 or wider, within the bound.
A program may use at most 64 MiB of HBM per device.

v0:
```python
import functools

import jax
import jax.numpy as jnp
from jax import lax
from jax.experimental import pallas as pl
from jax.experimental.pallas import tpu as pltpu
from jax.sharding import PartitionSpec as P

D = 256
H = 8
DH = 32
TILE = 128
CAP = 3


def normalize(rows):
    rows = rows.astype(jnp.float32)
    centre = rows - jnp.mean(rows, axis=-1, keepdims=True)
    return centre * lax.rsqrt(jnp.mean(centre * centre, axis=-1, keepdims=True) + 1e-05)


def feature(values):
    return jax.nn.elu(values) + 1.0


def fetch_rows(expert_in, expert_out):
    return (
        lax.all_gather(expert_in, ("pb", "kv"), axis=1, tiled=True),
        lax.all_gather(expert_out, ("pb", "kv"), axis=1, tiled=True),
    )


def body(
    queries, coords, inputs, w_query, w_key, w_value, w_out, expert_in, expert_out, gate_geo, routes
):
    high = lax.Precision.HIGHEST
    query_rows = queries[0]
    count = query_rows.shape[0]
    tiles_here = count // TILE
    normed_in = normalize(inputs[0]).astype(jnp.bfloat16)
    points = normed_in.shape[0]
    keys = feature(jnp.dot(normed_in, w_key, preferred_element_type=jnp.float32)).reshape(
        points, H, DH
    )
    vals = jnp.dot(normed_in, w_value, preferred_element_type=jnp.float32).reshape(points, H, DH)
    memory, ksum = lax.psum(
        (jnp.einsum("nhi,nhj->hij", keys, vals, precision=high), jnp.sum(keys, axis=0)), "kv"
    )
    normed_q = normalize(query_rows).astype(jnp.bfloat16)
    qfeat = feature(jnp.dot(normed_q, w_query, preferred_element_type=jnp.float32)).reshape(
        count, H, DH
    )
    numer = jnp.einsum("nhi,hij->nhj", qfeat, memory, precision=high)
    denom = jnp.einsum("nhi,hi->nh", qfeat, ksum, precision=high)
    attn = (numer / denom[:, :, None]).reshape(count, D).astype(jnp.bfloat16)
    resid = (
        query_rows.astype(jnp.float32) + jnp.dot(attn, w_out, preferred_element_type=jnp.float32)
    ).astype(jnp.bfloat16)
    experts = routes[0, :, 0]
    total_experts = gate_geo.shape[0]
    served = expert_in.shape[0]
    owners = total_experts // served
    onehot = (experts[:, None] == jnp.arange(total_experts, dtype=jnp.int32)[None, :]).astype(
        jnp.int32
    )
    before = jnp.cumsum(onehot, axis=0) - onehot
    rank = jnp.sum(before * onehot, axis=1)
    slot = experts * CAP + rank
    slots_all = total_experts * CAP
    select = (slot[None, :] == jnp.arange(slots_all, dtype=jnp.int32)[:, None]).astype(jnp.bfloat16)
    packed = jnp.dot(
        select, resid.reshape(tiles_here, TILE * D), preferred_element_type=jnp.float32
    ).astype(jnp.bfloat16)
    received = lax.all_to_all(packed, "ex", split_axis=0, concat_axis=0, tiled=True)
    arranged = received.reshape(owners, served, CAP * TILE, D)
    first_layer, second_layer = fetch_rows(expert_in, expert_out)
    outputs = []
    for local in range(served):
        rows = arranged[:, local].reshape(owners * CAP * TILE, D)
        rows = normalize(rows).astype(jnp.bfloat16)
        hidden = jax.nn.gelu(
            jnp.dot(rows, first_layer[local], preferred_element_type=jnp.float32), approximate=False
        ).astype(jnp.bfloat16)
        answer = jnp.dot(hidden, second_layer[local], preferred_element_type=jnp.float32).astype(
            jnp.bfloat16
        )
        outputs.append(answer.reshape(owners, 1, CAP * TILE, D))
    served_out = jnp.concatenate(outputs, axis=1).reshape(slots_all, TILE * D)
    returned = lax.all_to_all(served_out, "ex", split_axis=0, concat_axis=0, tiled=True)
    ffn = jnp.dot(jnp.transpose(select), returned, preferred_element_type=jnp.float32).reshape(
        count, D
    )
    coeff = jnp.dot(onehot.astype(jnp.float32), gate_geo, precision=high)
    logit = jnp.sum(
        coords[0].reshape(3, tiles_here, TILE) * jnp.transpose(coeff)[:, :, None], axis=0
    ).reshape(count)
    gate = jax.nn.sigmoid(logit)
    result = (resid.astype(jnp.float32) + gate[:, None] * ffn).astype(jnp.bfloat16)
    return result[None]


def gelu_exact(x):
    size = jnp.abs(x)
    t = 1.0 / (1.0 + 0.2316418882663604 * size)
    poly = t * (
        0.127414796 + t * (-0.142248368 + t * (0.710706871 + t * (-0.726576014 + t * 0.530702715)))
    )
    return jnp.maximum(x, 0.0) - size * poly * jnp.exp(-0.5 * x * x)


def phi(t):
    return jnp.where(t > 0.0, t + 1.0, jnp.exp(jnp.minimum(t, 0.0)))


def row_norm(rows):
    rows = rows.astype(jnp.float32)
    width = rows.shape[-1]
    centre = rows - jnp.sum(rows, axis=-1, keepdims=True) * (1.0 / width)
    var = jnp.sum(centre * centre, axis=-1, keepdims=True) * (1.0 / width)
    return (centre * lax.rsqrt(var + 1e-05)).astype(jnp.bfloat16)


def dot32(a, b):
    return jnp.dot(a, b, preferred_element_type=jnp.float32)


def fused(
    npb, nkv, nex,
    q_ref, coords_ref, in_ref, wq_ref, wk_ref, wv_ref, wo_ref, ein_ref, eout_ref, geo_ref, routes_ref,
    o_ref,
    w1, w2, qf, resid, normed, hidden, msg, kvbd, ksum,
    own_sem, zs, zr, ys, yr, xs, xr, fxs, fxr, fys, fyr, cs, cr, ms, mr,
):
    P_, Z, X = lax.axis_index("pb"), lax.axis_index("kv"), lax.axis_index("ex")
    py = lax.rem(P_ + 2, 4)
    pc = P_ + 1 - 2 * lax.rem(P_, 2)
    pcy = lax.rem(pc + 2, 4)
    xn = 1 - X
    bufs, srcs = (w1, w2), (ein_ref, eout_ref)
    served = ein_ref.shape[0]
    hs = served // 2
    to_y, to_x, to_c = {"pb": py}, {"ex": xn}, {"pb": pc}

    def block(m, x, p, z, half=None):
        if half is None:
            return bufs[m].at[pl.ds(x * served, served), p, z]
        return bufs[m].at[pl.ds(x * served + half * hs, hs), p, z]

    def rcopy(src, dst, s, r, dev):
        return pltpu.make_async_remote_copy(
            src_ref=src, dst_ref=dst, send_sem=s, recv_sem=r,
            device_id=dev, device_id_type=pl.DeviceIdType.MESH,
        )

    def zof(d):
        return lax.rem(Z + nkv - d, nkv)

    barrier = pltpu.get_barrier_semaphore()
    partners = [to_y, to_x, to_c] + [{"kv": lax.rem(Z + d, nkv)} for d in range(1, nkv)]
    for dev in partners:
        pl.semaphore_signal(barrier, inc=1, device_id=dev, device_id_type=pl.DeviceIdType.MESH)
    pl.semaphore_wait(barrier, len(partners))

    def own_copy(m):
        return pltpu.make_async_copy(srcs[m], block(m, X, P_, Z), own_sem.at[m])

    def z_copy(m, d):
        return rcopy(srcs[m], block(m, X, P_, Z), zs.at[m, d], zr.at[m, d], {"kv": lax.rem(Z + d, nkv)})

    def z_arrive(m, d):
        b = block(m, X, P_, zof(d))
        return rcopy(b, b, zs.at[m, d], zr.at[m, d], {"kv": lax.rem(Z + d, nkv)})

    def pair(m, x, p, d, s, r, dev, half=None, src=None):
        b = block(m, x, p, zof(d), half)
        return rcopy(b if src is None else src, b, s.at[m, d], r.at[m, d], dev)

    def core(m, k, d, src=None):
        x, p = ((X, P_), (X, py), (xn, P_), (xn, py))[k]
        b = block(m, x, p, zof(d))
        return rcopy(b if src is None else src, b, cs.at[m, k, d], cr.at[m, k, d], to_c)

    def core_arrive(m, k, d):
        x, p = ((X, pc), (X, pcy), (xn, pc), (xn, pcy))[k]
        b = block(m, x, p, zof(d))
        return rcopy(b, b, cs.at[m, k, d], cr.at[m, k, d], to_c)

    def start_z(m):
        own_copy(m).start()
        for d in range(1, nkv):
            z_copy(m, d).start()

    def start_xy(m):
        pair(m, X, P_, 0, xs, xr, to_x, src=srcs[m]).start()
        pair(m, X, P_, 0, ys, yr, to_y, src=srcs[m]).start()
        core(m, 0, 0, src=srcs[m]).start()

    def f1(m, d):
        z_arrive(m, d).wait_recv()
        pair(m, X, P_, d, xs, xr, to_x).start()
        pair(m, X, P_, d, ys, yr, to_y).start()
        core(m, 0, d).start()

    def f2(m, d):
        pair(m, X, py, d, ys, yr, to_y).wait_recv()
        pair(m, X, py, d, fxs, fxr, to_x, half=0).start()
        core(m, 1, d).start()
        pair(m, xn, P_, d, xs, xr, to_x).wait_recv()
        pair(m, xn, P_, d, fys, fyr, to_y, half=1).start()
        core(m, 2, d).start()

    def f3(m, d):
        pair(m, xn, py, d, fxs, fxr, to_x, half=0).wait_recv()
        pair(m, xn, py, d, fys, fyr, to_y, half=1).wait_recv()
        core(m, 3, d).start()

    def arrive_all(m):
        own_copy(m).wait()
        for d in range(nkv):
            for k in range(4):
                core_arrive(m, k, d).wait_recv()

    def sent_all(m):
        for d in range(nkv):
            if d:
                z_copy(m, d).wait_send()
            pair(m, X, P_, d, xs, xr, to_x).wait_send()
            pair(m, X, P_, d, ys, yr, to_y).wait_send()
            pair(m, X, py, d, fxs, fxr, to_x, half=0).wait_send()
            pair(m, xn, P_, d, fys, fyr, to_y, half=1).wait_send()
            for k in range(4):
                core(m, k, d).wait_send()

    start_z(0)
    start_xy(0)

    width = q_ref.shape[1]
    nin = row_norm(in_ref[...])
    keys = phi(dot32(nin, wk_ref[...]))
    vals = dot32(nin, wv_ref[...])
    keys_b, vals_b = keys.astype(jnp.bfloat16), vals.astype(jnp.bfloat16)
    lane = lax.broadcasted_iota(jnp.int32, (DH, 128), 1) // DH
    per = 128 // DH
    rows_kv = DH * (width // 128)
    for t in range(width // 128):
        cols = slice(128 * t, 128 * (t + 1))
        mem = lax.dot_general(
            keys_b[:, cols], vals_b[:, cols], (((0,), (0,)), ((), ())),
            preferred_element_type=jnp.float32,
        )
        total = jnp.zeros((DH, 128), jnp.float32)
        for h in range(per):
            total = jnp.where(lane == h, mem[h * DH : (h + 1) * DH], total)
        msg[0, DH * t : DH * (t + 1), :] = total
        sums = jnp.sum(keys[:, cols], axis=0, keepdims=True)
        msg[0, rows_kv + 8 * t : rows_kv + 8 * (t + 1), :] = jnp.broadcast_to(sums, (8, 128))

    def m_copy(d):
        return rcopy(msg.at[0], msg.at[d], ms.at[d], mr.at[d], {"kv": lax.rem(Z + d, nkv)})

    for d in range(1, nkv):
        m_copy(d).start()

    count = q_ref.shape[0]
    step = 256
    chunks = count // step

    def q_stage(lo, hi):
        @pl.loop(lo, hi)
        def _(i):
            rows = pl.ds(pl.multiple_of(i * step, step), step)
            qf[rows, :] = phi(dot32(row_norm(q_ref[rows, :]), wq_ref[...])).astype(jnp.bfloat16)

    part = chunks // 4
    f1(0, 1)
    q_stage(0, part)
    f1(0, 2)
    f2(0, 0)
    q_stage(part, 2 * part)
    f1(0, 3)
    start_z(1)
    f2(0, 1)
    q_stage(2 * part, chunks)

    for d in range(1, nkv):
        m_copy(d).wait_recv()
    both = msg[0]
    for d in range(1, nkv):
        both = both + msg[d]
    kvbd[...] = jnp.zeros_like(kvbd)
    for t in range(width // 128):
        mem = both[DH * t : DH * (t + 1)]
        for h in range(per):
            r0 = 128 * t + DH * h
            kvbd[r0 : r0 + DH, 128 * t : 128 * (t + 1)] = jnp.where(lane == h, mem, 0.0).astype(jnp.bfloat16)
        ksum[:, 128 * t : 128 * (t + 1)] = both[rows_kv + 8 * t : rows_kv + 8 * (t + 1)]
    same = (
        lax.broadcasted_iota(jnp.int32, (width, width), 0) // DH
        == lax.broadcasted_iota(jnp.int32, (width, width), 1) // DH
    ).astype(jnp.float32).astype(jnp.bfloat16)

    def attn_stage(lo, hi):
        @pl.loop(lo, hi)
        def _(i):
            rows = pl.ds(pl.multiple_of(i * step, step), step)
            f = qf[rows, :]
            numer = dot32(f, kvbd[...])
            denom = dot32((f.astype(jnp.float32) * ksum[0:1, :]).astype(jnp.bfloat16), same)
            attn = (numer / denom).astype(jnp.bfloat16)
            r = (q_ref[rows, :].astype(jnp.float32) + dot32(attn, wo_ref[...])).astype(jnp.bfloat16)
            resid[rows, :] = r
            normed[rows, :] = row_norm(r)

    attn_stage(0, part)
    f3(0, 0)
    f2(0, 2)
    attn_stage(part, 2 * part)
    f3(0, 1)
    f2(0, 3)
    start_xy(1)
    attn_stage(2 * part, chunks)
    f3(0, 2)
    f3(0, 3)
    f1(1, 1)
    arrive_all(0)

    tiles = count // TILE
    fdim = hidden.shape[1]
    wide = 256

    def up_stage(lo, hi):
        @pl.loop(lo, hi)
        def _(i):
            rows = pl.ds(pl.multiple_of(i * TILE, TILE), TILE)
            e = routes_ref[i, 0]
            x = normed[rows, :]
            for c in range(fdim // wide):
                w = w1[e, :, :, :, c * wide : (c + 1) * wide].reshape(width, wide)
                hidden[rows, c * wide : (c + 1) * wide] = gelu_exact(dot32(x, w)).astype(jnp.bfloat16)

    quarter = tiles // 8
    up_stage(0, quarter)
    f1(1, 2)
    f2(1, 0)
    up_stage(quarter, 2 * quarter)
    f1(1, 3)
    f2(1, 1)
    up_stage(2 * quarter, 4 * quarter)
    f3(1, 0)
    f2(1, 2)
    up_stage(4 * quarter, 6 * quarter)
    f3(1, 1)
    f2(1, 3)
    up_stage(6 * quarter, tiles)
    f3(1, 2)
    f3(1, 3)
    arrive_all(1)

    @pl.loop(0, tiles)
    def _(i):
        start = pl.multiple_of(i * TILE, TILE)
        rows = pl.ds(start, TILE)
        e = routes_ref[i, 0]
        ffn = dot32(hidden[rows, :], w2[e].reshape(fdim, width)).astype(jnp.bfloat16).astype(jnp.float32)
        logit = coords_ref[0:1, rows] * geo_ref[e, 0]
        logit = logit + coords_ref[1:2, rows] * geo_ref[e, 1]
        logit = logit + coords_ref[2:3, rows] * geo_ref[e, 2]
        gate = 1.0 / (1.0 + jnp.exp(-logit))
        gate = jnp.transpose(jnp.broadcast_to(gate, (TILE, TILE)))
        gate = jnp.concatenate([gate] * (width // TILE), axis=1)
        o_ref[rows, :] = (resid[rows, :].astype(jnp.float32) + gate * ffn).astype(jnp.bfloat16)

    sent_all(0)
    sent_all(1)
    for d in range(1, nkv):
        m_copy(d).wait_send()


def fused_body(npb, nkv, nex, queries, coords, inputs, w_query, w_key, w_value, w_out, expert_in, expert_out, gate_geo, routes):
    count, width = queries.shape[1:]
    served, rows1, fdim = expert_in.shape
    rows2 = expert_out.shape[1]
    total = served * nex
    vmem = pl.BlockSpec(memory_space=pltpu.VMEM)
    smem = pl.BlockSpec(memory_space=pltpu.SMEM)
    hbm = pl.BlockSpec(memory_space=pl.ANY)
    dma = pltpu.SemaphoreType.DMA
    bf = jnp.bfloat16
    out = pl.pallas_call(
        functools.partial(fused, npb, nkv, nex),
        out_shape=jax.ShapeDtypeStruct((count, width), bf),
        in_specs=[vmem] * 7 + [hbm] * 2 + [smem] * 2,
        out_specs=vmem,
        scratch_shapes=[
            pltpu.VMEM((total, npb, nkv, rows1, fdim), bf),
            pltpu.VMEM((total, npb, nkv, rows2, width), bf),
            pltpu.VMEM((count, width), bf),
            pltpu.VMEM((count, width), bf),
            pltpu.VMEM((count, width), bf),
            pltpu.VMEM((count, fdim), bf),
            pltpu.VMEM((nkv, (DH + 8) * (width // 128), 128), jnp.float32),
            pltpu.VMEM((width, width), bf),
            pltpu.VMEM((8, width), jnp.float32),
            dma((2,)),
        ] + [dma((2, nkv))] * 10 + [dma((2, 4, nkv))] * 2 + [dma((nkv,))] * 2,
        compiler_params=pltpu.CompilerParams(collective_id=0, has_side_effects=True),
        name="fused",
    )(queries[0], coords[0], inputs[0], w_query, w_key, w_value, w_out, expert_in, expert_out, gate_geo, routes[0])
    return out[None]


def solution(mesh):
    in_specs = (
        P(("pb", "ex"), "kv", None),
        P(("pb", "ex"), None, "kv"),
        P(("pb", "ex"), "kv", None),
        P(),
        P(),
        P(),
        P(),
        P("ex", ("pb", "kv"), None),
        P("ex", ("pb", "kv"), None),
        P(),
        P(("pb", "ex"), "kv", None),
    )
    out_specs = P(("pb", "ex"), "kv", None)
    npb, nkv, nex = (mesh.shape[a] for a in ("pb", "kv", "ex"))
    chosen = functools.partial(fused_body, npb, nkv, nex) if (npb, nex) == (4, 2) else body
    return jax.shard_map(chosen, mesh=mesh, in_specs=in_specs, out_specs=out_specs, check_vma=False)
```

profile of v0, /device:TPU:25, one launch (start us, length us, event | category | flops | bytes accessed | tf_op | source)
XLA Modules:
  0.0 64.5 jit_solution(2521907199834881584)
XLA Ops:
  0.0 0.0 copy-start
  0.0 0.7 %copy-done = f32[8,3]{0,1:T(4,128)S(1)} copy-done((f32[8,3]{0,1:T(4,128)S(1)}, f32[8,3]{0,1:T(4,128)}, u32[]{:S(2)}) %copy-start) | copy-done | bytes 120
  0.7 0.0 copy-start.1
  0.7 0.7 %copy.12.geo_ref = f32[8,3]{1,0:T(8,128)} copy(f32[8,3]{0,1:T(4,128)S(1)} %copy-done) | data formatting | bytes 192 | tf_op args[9]
  1.4 0.0 copy-done.1
  1.4 0.7 %copy.13.routes_ref = s32[16,1]{1,0:T(8,128)} copy(s32[16,1]{0,1:T(1,128)S(1)} %bitcast.11) | data formatting | bytes 128 | tf_op jit(solution)/shard_map/squeeze | solution.py:409
  2.0 1.4 %copy.16 = f32[1,3,2048]{2,1,0:T(4,128)} copy(f32[1,3,2048]{2,0,1:T(1,128)} %param.12) | data formatting | bytes 49152
  3.4 58.9 %fused.1 = bf16[2048,256]{1,0:T(8,128)(2,1)} custom-call(bf16[2048,256]{1,0:T(8,128)(2,1)} %bitcast.8, f32[3,2048]{1,0:T(4,128)} %bitcast.10, bf16[512,256]{1,0:T(8,128)(2,1)} %bitcast.9, bf16[256,256]{1,0:T(8,128)(2,1)} %wq_ref.1, bf16[256,256]{1,0:T(8,128)(2,1)} %wk_ref.1, bf16[256,256]{1,0:T(8,128)(2,1)} %wv_ref.1, bf16[256,256]{1,0:T(8,128)(2,1)} %wo_ref.1, ...), custom_call_target="tpu_custom_call" | custom-call | tf_op jit(solution)/shard_map/fused/pallas_call | solution.py:390
  62.3 2.3 %copy.18 = bf16[1,2048,256]{2,1,0:T(8,128)(2,1)} copy(bf16[1,2048,256]{2,1,0:T(8,128)(2,1)} %bitcast.7) | data formatting | bytes 2097152
Async XLA Ops:
  0.0 0.7 %copy-start = (f32[8,3]{0,1:T(4,128)S(1)}, f32[8,3]{0,1:T(4,128)}, u32[]{:S(2)}) copy-start(f32[8,3]{0,1:T(4,128)} %param.20) | copy-start | bytes 292
  0.7 0.7 %copy-start.1 = (s32[1,16,1]{1,2,0:T(1,128)S(1)}, s32[1,16,1]{1,2,0:T(1,128)}, u32[]{:S(2)}) copy-start(s32[1,16,1]{1,2,0:T(1,128)} %param.21) | copy-start | bytes 196
where the time goes:
time: 64.8 us; the launch traced here: 64.5 us
  Pallas kernels  58.9 us (91%)
  local copies, waits for them, and re-layouts  5.66 us (9%)
    pallas_call x1, Pallas kernels, fused_body(): pl.pallas_call(functools.partial(fused, npb, nkv, nex), out_shape=jax.Sha...  58.9 us
    unnamed x7, local copies, waits for them, and re-layouts  4.98 us

commit v1 on v0

--- a/solution.py
+++ b/solution.py
@@ -127,25 +127,39 @@
 
 def fused(
     npb, nkv, nex,
-    q_ref, coords_ref, in_ref, wq_ref, wk_ref, wv_ref, wo_ref, ein_ref, eout_ref, geo_ref, routes_ref,
+    coords_ref, geo_ref, routes_ref, q_hbm, in_hbm, wq_hbm, wk_hbm, wv_hbm, wo_hbm, ein_ref, eout_ref,
     o_ref,
-    w1, w2, qf, resid, normed, hidden, msg, kvbd, ksum,
-    own_sem, zs, zr, ys, yr, xs, xr, fxs, fxr, fys, fyr, cs, cr, ms, mr,
+    q_ref, in_ref, wq_ref, wk_ref, wv_ref, wo_ref,
+    w1, w2own, w2oth, qf, resid, normed, hidden, acc, msg, kvbd, ksum,
+    load_sem, own_sem, ds_, dr_, zs, zr, ys, yr, xs, xr, fxs, fxr, fys, fyr, cs, cr, ms, mr,
 ):
     P_, Z, X = lax.axis_index("pb"), lax.axis_index("kv"), lax.axis_index("ex")
-    py = lax.rem(P_ + 2, 4)
-    pc = P_ + 1 - 2 * lax.rem(P_, 2)
-    pcy = lax.rem(pc + 2, 4)
+    mine, cb = P_ // 2, lax.rem(P_, 2)
+    cn = 1 - cb
     xn = 1 - X
-    bufs, srcs = (w1, w2), (ein_ref, eout_ref)
+    srcs = (ein_ref, eout_ref)
     served = ein_ref.shape[0]
     hs = served // 2
-    to_y, to_x, to_c = {"pb": py}, {"ex": xn}, {"pb": pc}
-
-    def block(m, x, p, z, half=None):
-        if half is None:
-            return bufs[m].at[pl.ds(x * served, served), p, z]
-        return bufs[m].at[pl.ds(x * served + half * hs, hs), p, z]
+    to_y, to_x, to_c = {"pb": lax.rem(P_ + 2, 4)}, {"ex": xn}, {"pb": 2 * mine + cn}
+
+    loads = [
+        pltpu.make_async_copy(src, dst, load_sem.at[k])
+        for k, (src, dst) in enumerate(
+            ((in_hbm, in_ref), (wk_hbm, wk_ref), (wv_hbm, wv_ref), (q_hbm, q_ref), (wq_hbm, wq_ref), (wo_hbm, wo_ref))
+        )
+    ]
+    for load in loads:
+        load.start()
+
+    def block(m, x, side, core_bit, z, half=None):
+        experts = pl.ds(x * served, served) if half is None else pl.ds(x * served + half * hs, hs)
+        if m:
+            return (w2own, w2oth)[side].at[experts, core_bit, z]
+        y = mine if side == 0 else 1 - mine
+        return w1.at[experts, 2 * y + core_bit, z]
+
+    def yblock(m, x, side, core_bit, z, half=None):
+        return block(m, x, 1 - side if m else side, core_bit, z, half)
 
     def rcopy(src, dst, s, r, dev):
         return pltpu.make_async_remote_copy(
@@ -163,28 +177,40 @@
     pl.semaphore_wait(barrier, len(partners))
 
     def own_copy(m):
-        return pltpu.make_async_copy(srcs[m], block(m, X, P_, Z), own_sem.at[m])
+        return pltpu.make_async_copy(srcs[m], block(m, X, 0, cb, Z), own_sem.at[m])
 
     def z_copy(m, d):
-        return rcopy(srcs[m], block(m, X, P_, Z), zs.at[m, d], zr.at[m, d], {"kv": lax.rem(Z + d, nkv)})
-
-    def z_arrive(m, d):
-        b = block(m, X, P_, zof(d))
-        return rcopy(b, b, zs.at[m, d], zr.at[m, d], {"kv": lax.rem(Z + d, nkv)})
-
-    def pair(m, x, p, d, s, r, dev, half=None, src=None):
-        b = block(m, x, p, zof(d), half)
-        return rcopy(b if src is None else src, b, s.at[m, d], r.at[m, d], dev)
+        return rcopy(srcs[m], block(m, X, 0, cb, Z), zs.at[m, d], zr.at[m, d], {"kv": lax.rem(Z + d, nkv)})
+
+    def diag_copy(m):
+        b = block(m, xn, 1, cb, Z)
+        return rcopy(b, b, ds_.at[m], dr_.at[m], {"kv": lax.rem(Z + 1, nkv)})
+
+    def arrive(m, x, side, core_bit, d, s, r, dev, half=None):
+        b = block(m, x, side, core_bit, zof(d), half)
+        rcopy(b, b, s, r, dev).wait_recv()
+
+    def to_x_copy(m, d, src=None):
+        b = block(m, X, 0, cb, zof(d))
+        return rcopy(b if src is None else src, b, xs.at[m, d], xr.at[m, d], to_x)
+
+    def to_y_copy(m, d, src=None):
+        b = block(m, X, 0, cb, zof(d))
+        return rcopy(b if src is None else src, yblock(m, X, 0, cb, zof(d)), ys.at[m, d], yr.at[m, d], to_y)
+
+    def on_x_copy(m, d):
+        b = block(m, X, 1, cb, zof(d), 0)
+        return rcopy(b, b, fxs.at[m, d], fxr.at[m, d], to_x)
+
+    def on_y_copy(m, d):
+        b = block(m, xn, 0, cb, zof(d), 1)
+        return rcopy(b, yblock(m, xn, 0, cb, zof(d), 1), fys.at[m, d], fyr.at[m, d], to_y)
+
+    kinds = ((X, 0), (X, 1), (xn, 0), (xn, 1))
 
     def core(m, k, d, src=None):
-        x, p = ((X, P_), (X, py), (xn, P_), (xn, py))[k]
-        b = block(m, x, p, zof(d))
+        b = block(m, *kinds[k], cb, zof(d))
         return rcopy(b if src is None else src, b, cs.at[m, k, d], cr.at[m, k, d], to_c)
-
-    def core_arrive(m, k, d):
-        x, p = ((X, pc), (X, pcy), (xn, pc), (xn, pcy))[k]
-        b = block(m, x, p, zof(d))
-        return rcopy(b, b, cs.at[m, k, d], cr.at[m, k, d], to_c)
 
     def start_z(m):
         own_copy(m).start()
@@ -192,43 +218,54 @@
             z_copy(m, d).start()
 
     def start_xy(m):
-        pair(m, X, P_, 0, xs, xr, to_x, src=srcs[m]).start()
-        pair(m, X, P_, 0, ys, yr, to_y, src=srcs[m]).start()
-        core(m, 0, 0, src=srcs[m]).start()
+        to_x_copy(m, 0, srcs[m]).start()
+        to_y_copy(m, 0, srcs[m]).start()
+        core(m, 0, 0, srcs[m]).start()
+
+    by_link = [d for d in range(nkv) if d != 1]
 
     def f1(m, d):
-        z_arrive(m, d).wait_recv()
-        pair(m, X, P_, d, xs, xr, to_x).start()
-        pair(m, X, P_, d, ys, yr, to_y).start()
+        arrive(m, X, 0, cb, d, zs.at[m, d], zr.at[m, d], {"kv": lax.rem(Z + d, nkv)})
+        to_x_copy(m, d).start()
+        to_y_copy(m, d).start()
         core(m, 0, d).start()
 
     def f2(m, d):
-        pair(m, X, py, d, ys, yr, to_y).wait_recv()
-        pair(m, X, py, d, fxs, fxr, to_x, half=0).start()
+        arrive(m, X, 1, cb, d, ys.at[m, d], yr.at[m, d], to_y)
+        if d in by_link:
+            on_x_copy(m, d).start()
         core(m, 1, d).start()
-        pair(m, xn, P_, d, xs, xr, to_x).wait_recv()
-        pair(m, xn, P_, d, fys, fyr, to_y, half=1).start()
+        arrive(m, xn, 0, cb, d, xs.at[m, d], xr.at[m, d], to_x)
+        if d in by_link:
+            on_y_copy(m, d).start()
         core(m, 2, d).start()
 
     def f3(m, d):
-        pair(m, xn, py, d, fxs, fxr, to_x, half=0).wait_recv()
-        pair(m, xn, py, d, fys, fyr, to_y, half=1).wait_recv()
+        if d in by_link:
+            arrive(m, xn, 1, cb, d, fxs.at[m, d], fxr.at[m, d], to_x, 0)
+            arrive(m, xn, 1, cb, d, fys.at[m, d], fyr.at[m, d], to_y, 1)
+        else:
+            arrive(m, xn, 1, cb, d, ds_.at[m], dr_.at[m], {"kv": lax.rem(Z + 1, nkv)})
+        if d == 0 and nkv > 1:
+            diag_copy(m).start()
         core(m, 3, d).start()
 
-    def arrive_all(m):
-        own_copy(m).wait()
+    def arrive_core(m, ks):
         for d in range(nkv):
-            for k in range(4):
-                core_arrive(m, k, d).wait_recv()
+            for k in ks:
+                arrive(m, *kinds[k], cn, d, cs.at[m, k, d], cr.at[m, k, d], to_c)
 
     def sent_all(m):
         for d in range(nkv):
             if d:
                 z_copy(m, d).wait_send()
-            pair(m, X, P_, d, xs, xr, to_x).wait_send()
-            pair(m, X, P_, d, ys, yr, to_y).wait_send()
-            pair(m, X, py, d, fxs, fxr, to_x, half=0).wait_send()
-            pair(m, xn, P_, d, fys, fyr, to_y, half=1).wait_send()
+            to_x_copy(m, d).wait_send()
+            to_y_copy(m, d).wait_send()
+            if d in by_link:
+                on_x_copy(m, d).wait_send()
+                on_y_copy(m, d).wait_send()
+            else:
+                diag_copy(m).wait_send()
             for k in range(4):
                 core(m, k, d).wait_send()
 
@@ -236,6 +273,8 @@
     start_xy(0)
 
     width = q_ref.shape[1]
+    for load in loads[:3]:
+        load.wait()
     nin = row_norm(in_ref[...])
     keys = phi(dot32(nin, wk_ref[...]))
     vals = dot32(nin, wv_ref[...])
@@ -272,16 +311,22 @@
             rows = pl.ds(pl.multiple_of(i * step, step), step)
             qf[rows, :] = phi(dot32(row_norm(q_ref[rows, :]), wq_ref[...])).astype(jnp.bfloat16)
 
+    for load in loads[3:]:
+        load.wait()
     part = chunks // 4
     f1(0, 1)
+    f2(0, 0)
     q_stage(0, part)
     f1(0, 2)
-    f2(0, 0)
+    f2(0, 1)
+    start_z(1)
     q_stage(part, 2 * part)
     f1(0, 3)
-    start_z(1)
-    f2(0, 1)
-    q_stage(2 * part, chunks)
+    start_xy(1)
+    q_stage(2 * part, 3 * part)
+    f3(0, 0)
+    f2(0, 2)
+    q_stage(3 * part, chunks)
 
     for d in range(1, nkv):
         m_copy(d).wait_recv()
@@ -313,17 +358,19 @@
             normed[rows, :] = row_norm(r)
 
     attn_stage(0, part)
-    f3(0, 0)
-    f2(0, 2)
+    f1(1, 1)
+    f2(0, 3)
     attn_stage(part, 2 * part)
     f3(0, 1)
-    f2(0, 3)
-    start_xy(1)
-    attn_stage(2 * part, chunks)
+    f2(1, 0)
+    attn_stage(2 * part, 3 * part)
+    f1(1, 2)
     f3(0, 2)
+    attn_stage(3 * part, chunks)
     f3(0, 3)
-    f1(1, 1)
-    arrive_all(0)
+    f2(1, 1)
+    own_copy(0).wait()
+    arrive_core(0, range(4))
 
     tiles = count // TILE
     fdim = hidden.shape[1]
@@ -333,43 +380,57 @@
         @pl.loop(lo, hi)
         def _(i):
             rows = pl.ds(pl.multiple_of(i * TILE, TILE), TILE)
-            e = routes_ref[i, 0]
+            e = routes_ref[0, i]
             x = normed[rows, :]
             for c in range(fdim // wide):
                 w = w1[e, :, :, :, c * wide : (c + 1) * wide].reshape(width, wide)
                 hidden[rows, c * wide : (c + 1) * wide] = gelu_exact(dot32(x, w)).astype(jnp.bfloat16)
 
-    quarter = tiles // 8
-    up_stage(0, quarter)
-    f1(1, 2)
-    f2(1, 0)
-    up_stage(quarter, 2 * quarter)
+    near = fdim // 2
+    near_cols = pl.ds(pl.multiple_of(mine * near, near), near)
+    far_cols = pl.ds(pl.multiple_of((1 - mine) * near, near), near)
+
+    def mid_stage(lo, hi):
+        @pl.loop(lo, hi)
+        def _(i):
+            rows = pl.ds(pl.multiple_of(i * TILE, TILE), TILE)
+            acc[rows, :] = dot32(hidden[rows, near_cols], w2own[routes_ref[0, i]].reshape(near, width))
+
+    part = tiles // 8
+    up_stage(0, part)
     f1(1, 3)
-    f2(1, 1)
-    up_stage(2 * quarter, 4 * quarter)
+    up_stage(part, 2 * part)
     f3(1, 0)
     f2(1, 2)
-    up_stage(4 * quarter, 6 * quarter)
+    up_stage(2 * part, 4 * part)
+    f2(1, 3)
+    up_stage(4 * part, 6 * part)
     f3(1, 1)
-    f2(1, 3)
-    up_stage(6 * quarter, tiles)
+    up_stage(6 * part, tiles)
     f3(1, 2)
+    own_copy(1).wait()
+    arrive_core(1, (0, 2))
+    mid_stage(0, tiles // 2)
     f3(1, 3)
-    arrive_all(1)
-
-    @pl.loop(0, tiles)
-    def _(i):
-        start = pl.multiple_of(i * TILE, TILE)
-        rows = pl.ds(start, TILE)
-        e = routes_ref[i, 0]
-        ffn = dot32(hidden[rows, :], w2[e].reshape(fdim, width)).astype(jnp.bfloat16).astype(jnp.float32)
-        logit = coords_ref[0:1, rows] * geo_ref[e, 0]
-        logit = logit + coords_ref[1:2, rows] * geo_ref[e, 1]
-        logit = logit + coords_ref[2:3, rows] * geo_ref[e, 2]
-        gate = 1.0 / (1.0 + jnp.exp(-logit))
-        gate = jnp.transpose(jnp.broadcast_to(gate, (TILE, TILE)))
-        gate = jnp.concatenate([gate] * (width // TILE), axis=1)
-        o_ref[rows, :] = (resid[rows, :].astype(jnp.float32) + gate * ffn).astype(jnp.bfloat16)
+    mid_stage(tiles // 2, tiles)
+    arrive_core(1, (1, 3))
+
+    def down_stage(lo, hi):
+        @pl.loop(lo, hi)
+        def _(i):
+            start = pl.multiple_of(i * TILE, TILE)
+            rows = pl.ds(start, TILE)
+            e = routes_ref[0, i]
+            ffn = (acc[rows, :] + dot32(hidden[rows, far_cols], w2oth[e].reshape(near, width))).astype(jnp.bfloat16).astype(jnp.float32)
+            logit = coords_ref[0, 0:1, rows] * geo_ref[0, e]
+            logit = logit + coords_ref[1, 0:1, rows] * geo_ref[1, e]
+            logit = logit + coords_ref[2, 0:1, rows] * geo_ref[2, e]
+            gate = 1.0 / (1.0 + jnp.exp(-logit))
+            gate = jnp.transpose(jnp.broadcast_to(gate, (TILE, TILE)))
+            gate = jnp.concatenate([gate] * (width // TILE), axis=1)
+            o_ref[rows, :] = (resid[rows, :].astype(jnp.float32) + gate * ffn).astype(jnp.bfloat16)
+
+    down_stage(0, tiles)
 
     sent_all(0)
     sent_all(1)
@@ -390,23 +451,31 @@
     out = pl.pallas_call(
         functools.partial(fused, npb, nkv, nex),
         out_shape=jax.ShapeDtypeStruct((count, width), bf),
-        in_specs=[vmem] * 7 + [hbm] * 2 + [smem] * 2,
+        in_specs=[vmem] + [smem] * 2 + [hbm] * 8,
         out_specs=vmem,
         scratch_shapes=[
+            pltpu.VMEM((count, width), bf),
+            pltpu.VMEM(inputs.shape[1:], bf),
+        ] + [pltpu.VMEM((width, width), bf)] * 4 + [
             pltpu.VMEM((total, npb, nkv, rows1, fdim), bf),
-            pltpu.VMEM((total, npb, nkv, rows2, width), bf),
+            pltpu.VMEM((total, npb // 2, nkv, rows2, width), bf),
+            pltpu.VMEM((total, npb // 2, nkv, rows2, width), bf),
             pltpu.VMEM((count, width), bf),
             pltpu.VMEM((count, width), bf),
             pltpu.VMEM((count, width), bf),
             pltpu.VMEM((count, fdim), bf),
+            pltpu.VMEM((count, width), jnp.float32),
             pltpu.VMEM((nkv, (DH + 8) * (width // 128), 128), jnp.float32),
             pltpu.VMEM((width, width), bf),
             pltpu.VMEM((8, width), jnp.float32),
-            dma((2,)),
-        ] + [dma((2, nkv))] * 10 + [dma((2, 4, nkv))] * 2 + [dma((nkv,))] * 2,
+            dma((6,)),
+        ] + [dma((2,))] * 3 + [dma((2, nkv))] * 10 + [dma((2, 4, nkv))] * 2 + [dma((nkv,))] * 2,
         compiler_params=pltpu.CompilerParams(collective_id=0, has_side_effects=True),
         name="fused",
-    )(queries[0], coords[0], inputs[0], w_query, w_key, w_value, w_out, expert_in, expert_out, gate_geo, routes[0])
+    )(
+        jnp.transpose(coords, (1, 0, 2)), jnp.transpose(gate_geo), routes[:, :, 0],
+        queries[0], inputs[0], w_query, w_key, w_value, w_out, expert_in, expert_out,
+    )
     return out[None]
 
 

time: 64.8 us -> 59.3 us (0.915)
  the two profiles are of different devices: /device:TPU:25 before, /device:TPU:19 now
where the time goes in v1:
time: 59.3 us; the launch traced here: 59.1 us
  Pallas kernels  56.8 us (96%)
  local copies, waits for them, and re-layouts  2.26 us (4%)
    pallas_call x1, Pallas kernels, fused_body(): pl.pallas_call(functools.partial(fused, npb, nkv, nex), out_shape=jax.Sha...  56.8 us
    unnamed x1, local copies, waits for them, and re-layouts  2.26 us

profile of v1, /device:TPU:19, one launch (start us, length us, event | category | flops | bytes accessed | tf_op | source)
XLA Modules:
  0.0 59.1 jit_solution(10437256553937280158)
XLA Ops:
  0.0 56.8 %fused.1 = bf16[2048,256]{1,0:T(8,128)(2,1)} custom-call(f32[3,1,2048]{2,1,0:T(1,128)} %bitcast.9, f32[3,8]{1,0:T(4,128)} %bitcast.10, s32[1,16]{1,0:T(1,128)} %bitcast.11, bf16[2048,256]{1,0:T(8,128)(2,1)} %bitcast.7, bf16[512,256]{1,0:T(8,128)(2,1)} %bitcast.8, bf16[256,256]{1,0:T(8,128)(2,1)} %wq_hbm.1, bf16[256,256]{1,0:T(8,128)(2,1)} %wk_hbm.1, ...), custom_call_target="tpu_custom_call" | custom-call | tf_op jit(solution)/shard_map/fused/pallas_call | solution.py:451
  56.8 2.3 %copy.13 = bf16[1,2048,256]{2,1,0:T(8,128)(2,1)} copy(bf16[1,2048,256]{2,1,0:T(8,128)(2,1)} %bitcast.6) | data formatting | bytes 2097152

commit v2 on v1

--- a/solution.py
+++ b/solution.py
@@ -131,7 +131,7 @@
     o_ref,
     q_ref, in_ref, wq_ref, wk_ref, wv_ref, wo_ref,
     w1, w2own, w2oth, qf, resid, normed, hidden, acc, msg, kvbd, ksum,
-    load_sem, own_sem, ds_, dr_, zs, zr, ys, yr, xs, xr, fxs, fxr, fys, fyr, cs, cr, ms, mr,
+    load_sem, own_sem, zs, zr, ys, yr, xs, xr, fxs, fxr, fys, fyr, cs, cr, ms, mr,
 ):
     P_, Z, X = lax.axis_index("pb"), lax.axis_index("kv"), lax.axis_index("ex")
     mine, cb = P_ // 2, lax.rem(P_, 2)
@@ -182,10 +182,6 @@
     def z_copy(m, d):
         return rcopy(srcs[m], block(m, X, 0, cb, Z), zs.at[m, d], zr.at[m, d], {"kv": lax.rem(Z + d, nkv)})
 
-    def diag_copy(m):
-        b = block(m, xn, 1, cb, Z)
-        return rcopy(b, b, ds_.at[m], dr_.at[m], {"kv": lax.rem(Z + 1, nkv)})
-
     def arrive(m, x, side, core_bit, d, s, r, dev, half=None):
         b = block(m, x, side, core_bit, zof(d), half)
         rcopy(b, b, s, r, dev).wait_recv()
@@ -221,8 +217,6 @@
         to_x_copy(m, 0, srcs[m]).start()
         to_y_copy(m, 0, srcs[m]).start()
         core(m, 0, 0, srcs[m]).start()
-
-    by_link = [d for d in range(nkv) if d != 1]
 
     def f1(m, d):
         arrive(m, X, 0, cb, d, zs.at[m, d], zr.at[m, d], {"kv": lax.rem(Z + d, nkv)})
@@ -232,22 +226,15 @@
 
     def f2(m, d):
         arrive(m, X, 1, cb, d, ys.at[m, d], yr.at[m, d], to_y)
-        if d in by_link:
-            on_x_copy(m, d).start()
+        on_x_copy(m, d).start()
         core(m, 1, d).start()
         arrive(m, xn, 0, cb, d, xs.at[m, d], xr.at[m, d], to_x)
-        if d in by_link:
-            on_y_copy(m, d).start()
+        on_y_copy(m, d).start()
         core(m, 2, d).start()
 
     def f3(m, d):
-        if d in by_link:
-            arrive(m, xn, 1, cb, d, fxs.at[m, d], fxr.at[m, d], to_x, 0)
-            arrive(m, xn, 1, cb, d, fys.at[m, d], fyr.at[m, d], to_y, 1)
-        else:
-            arrive(m, xn, 1, cb, d, ds_.at[m], dr_.at[m], {"kv": lax.rem(Z + 1, nkv)})
-        if d == 0 and nkv > 1:
-            diag_copy(m).start()
+        arrive(m, xn, 1, cb, d, fxs.at[m, d], fxr.at[m, d], to_x, 0)
+        arrive(m, xn, 1, cb, d, fys.at[m, d], fyr.at[m, d], to_y, 1)
         core(m, 3, d).start()
 
     def arrive_core(m, ks):
@@ -261,11 +248,8 @@
                 z_copy(m, d).wait_send()
             to_x_copy(m, d).wait_send()
             to_y_copy(m, d).wait_send()
-            if d in by_link:
-                on_x_copy(m, d).wait_send()
-                on_y_copy(m, d).wait_send()
-            else:
-                diag_copy(m).wait_send()
+            on_x_copy(m, d).wait_send()
+            on_y_copy(m, d).wait_send()
             for k in range(4):
                 core(m, k, d).wait_send()
 
@@ -369,6 +353,7 @@
     attn_stage(3 * part, chunks)
     f3(0, 3)
     f2(1, 1)
+    f1(1, 3)
     own_copy(0).wait()
     arrive_core(0, range(4))
 
@@ -398,16 +383,16 @@
 
     part = tiles // 8
     up_stage(0, part)
-    f1(1, 3)
+    f3(1, 0)
     up_stage(part, 2 * part)
-    f3(1, 0)
     f2(1, 2)
     up_stage(2 * part, 4 * part)
     f2(1, 3)
-    up_stage(4 * part, 6 * part)
+    up_stage(4 * part, 5 * part)
     f3(1, 1)
+    up_stage(5 * part, 6 * part)
+    f3(1, 2)
     up_stage(6 * part, tiles)
-    f3(1, 2)
     own_copy(1).wait()
     arrive_core(1, (0, 2))
     mid_stage(0, tiles // 2)
@@ -469,7 +454,7 @@
             pltpu.VMEM((width, width), bf),
             pltpu.VMEM((8, width), jnp.float32),
             dma((6,)),
-        ] + [dma((2,))] * 3 + [dma((2, nkv))] * 10 + [dma((2, 4, nkv))] * 2 + [dma((nkv,))] * 2,
+        ] + [dma((2,))] + [dma((2, nkv))] * 10 + [dma((2, 4, nkv))] * 2 + [dma((nkv,))] * 2,
         compiler_params=pltpu.CompilerParams(collective_id=0, has_side_effects=True),
         name="fused",
     )(

time: 59.3 us -> 58.1 us (0.980)
  the two profiles are of different devices: /device:TPU:19 before, /device:TPU:25 now
where the time goes in v2:
time: 58.1 us; the launch traced here: 57.8 us
  Pallas kernels  55.5 us (96%)
  local copies, waits for them, and re-layouts  2.26 us (4%)
    pallas_call x1, Pallas kernels, fused_body(): pl.pallas_call(functools.partial(fused, npb, nkv, nex), out_shape=jax.Sha...  55.5 us
    unnamed x1, local copies, waits for them, and re-layouts  2.26 us

profile of v2, /device:TPU:25, one launch (start us, length us, event | category | flops | bytes accessed | tf_op | source)
XLA Modules:
  0.0 57.8 jit_solution(12108320749135110753)
XLA Ops:
  0.0 55.5 %fused.1 = bf16[2048,256]{1,0:T(8,128)(2,1)} custom-call(f32[3,1,2048]{2,1,0:T(1,128)} %bitcast.9, f32[3,8]{1,0:T(4,128)} %bitcast.10, s32[1,16]{1,0:T(1,128)} %bitcast.11, bf16[2048,256]{1,0:T(8,128)(2,1)} %bitcast.7, bf16[512,256]{1,0:T(8,128)(2,1)} %bitcast.8, bf16[256,256]{1,0:T(8,128)(2,1)} %wq_hbm.1, bf16[256,256]{1,0:T(8,128)(2,1)} %wk_hbm.1, ...), custom_call_target="tpu_custom_call" | custom-call | tf_op jit(solution)/shard_map/fused/pallas_call | solution.py:436
  55.5 2.3 %copy.13 = bf16[1,2048,256]{2,1,0:T(8,128)(2,1)} copy(bf16[1,2048,256]{2,1,0:T(8,128)(2,1)} %bitcast.6) | data formatting | bytes 2097152
